TPU v7x, 128 devices: a whole 4x4x4 slice. The times are simulated.
128 devices in a mesh: chan: 16 (over z, x_hi, core), win: 8 (over y, x_lo).
Axes of the slice: x: 4 (x_hi: 2, x_lo: 2; x = x_hi * 2 + x_lo), y: 4, z: 4, core: 2. Of those that a mesh axis runs over, the one named last changes fastest.
Arguments:
- series: bfloat16 [64, 2048, 1500], P('win', 'chan'), may hold values from -1700 to 1700
- validity: int32 [64, 2048], P('win', 'chan'), may hold values from 0 to 1, as said below
Outputs:
- source_gathers: float32 [2048, 16, 8, 16, 128], P('chan', None, 'win')
Inputs may be any that keep to these rules, and one draw needn't show every extreme that they name: `validity`: a channel flagged dead is 0 in every window.
All inputs are finite; a program needn't handle non-finite values.
Results may differ from a plain program's by a relative error of at most 0.0037.
Values may be sent and summed in bfloat16 or wider, within the bound.
No kernel may reach another device: no remote copies, remote signals or barrier semaphores. Data moves between devices by JAX's collectives and lax.ppermute only.
A program may use at most 192 MiB of HBM per device.

v0:
```python
import math
import jax
import jax.numpy as jnp
from jax import lax
from jax.sharding import PartitionSpec as P

CHANNELS = 2048
SAMPLES = 1500
BINS = 128
LAGS = 128
SOURCES = 2048
lowest_bin = 6


def build_tables():
    sample_idx = jnp.arange(SAMPLES, dtype=jnp.int32)
    bin_idx = jnp.arange(BINS, dtype=jnp.int32) + lowest_bin
    phase_index = sample_idx[:, None] * bin_idx[None, :] % SAMPLES
    phase_angle = phase_index.astype(jnp.float32) * (2.0 * math.pi / SAMPLES)
    hann_taper = 0.5 - 0.5 * jnp.cos(sample_idx.astype(jnp.float32) * (2.0 * math.pi / SAMPLES))
    taper_table = jnp.concatenate(
        [hann_taper[:, None] * jnp.cos(phase_angle), -hann_taper[:, None] * jnp.sin(phase_angle)],
        axis=1,
    ).astype(jnp.bfloat16)
    lag_idx = jnp.arange(LAGS, dtype=jnp.int32) - LAGS // 2
    lag_index = bin_idx[:, None] * lag_idx[None, :] % SAMPLES
    lag_angle = lag_index.astype(jnp.float32) * (2.0 * math.pi / SAMPLES)
    inverse = jnp.concatenate([jnp.cos(lag_angle), -jnp.sin(lag_angle)], axis=0)
    return (taper_table, inverse)


def pair_block(src_spec, src_flags, recv_spec, recv_flags, inverse):
    src_real = src_spec[..., :BINS]
    src_imag = src_spec[..., BINS:]
    recv_real = recv_spec[..., :BINS]
    recv_imag = recv_spec[..., BINS:]
    in_phase = jnp.einsum("wsk,wik->sik", src_real, recv_real, preferred_element_type=jnp.float32)
    in_phase = in_phase + jnp.einsum(
        "wsk,wik->sik", src_imag, recv_imag, preferred_element_type=jnp.float32
    )
    quadrature = jnp.einsum("wsk,wik->sik", src_real, recv_imag, preferred_element_type=jnp.float32)
    quadrature = quadrature - jnp.einsum(
        "wsk,wik->sik", src_imag, recv_real, preferred_element_type=jnp.float32
    )
    joined = jnp.concatenate([in_phase, quadrature], axis=-1)
    lead_rows, recv_rows, spec_width = joined.shape
    lagged = jnp.dot(
        joined.reshape(lead_rows * recv_rows, spec_width),
        inverse,
        precision=lax.Precision.HIGHEST,
        preferred_element_type=jnp.float32,
    )
    lagged = lagged.reshape(lead_rows, recv_rows, LAGS)
    pair_count = jnp.einsum("ws,wi->si", src_flags, recv_flags, preferred_element_type=jnp.float32)
    return (lagged, pair_count)


def on_device(series, validity):
    win_rows, channel_count, samples = series.shape
    taper_table, inverse = build_tables()
    spectra = jnp.dot(
        series.reshape(win_rows * channel_count, samples),
        taper_table,
        preferred_element_type=jnp.float32,
    )
    spectra = spectra.reshape(win_rows, channel_count, 2 * BINS)
    energy = jnp.mean(spectra * spectra, axis=-1, keepdims=True)
    flag_float = validity.astype(jnp.float32)
    whitened = (spectra * lax.rsqrt(energy + 1e-06) * flag_float[..., None]).astype(jnp.bfloat16)
    flag_half = validity.astype(jnp.bfloat16)
    stride = CHANNELS // SOURCES
    src_spec, src_flags = (
        lax.all_gather(whitened, "win", axis=0, tiled=True),
        lax.all_gather(flag_half, "win", axis=0, tiled=True),
    )
    blocks = lax.axis_size("chan")
    slot_count = lax.axis_size("win")
    slot_width = channel_count // slot_count
    own_sources = src_spec.shape[1]
    every_spec, every_flags = (
        lax.all_gather(whitened, "chan", axis=1, tiled=True),
        lax.all_gather(flag_half, "chan", axis=1, tiled=True),
    )
    every_spec = every_spec.reshape(win_rows, blocks, slot_count, slot_width, 2 * BINS)
    every_flags = every_flags.reshape(win_rows, blocks, slot_count, slot_width)
    recv_spec, recv_flags = (
        lax.all_to_all(every_spec, "win", split_axis=2, concat_axis=0, tiled=True),
        lax.all_to_all(every_flags, "win", split_axis=2, concat_axis=0, tiled=True),
    )
    recv_spec = recv_spec.reshape(win_rows * slot_count, blocks * slot_width, 2 * BINS)
    recv_flags = recv_flags.reshape(win_rows * slot_count, blocks * slot_width)
    stacked, pair_count = pair_block(src_spec, src_flags, recv_spec, recv_flags, inverse)
    result = stacked / jnp.maximum(pair_count, 1.0)[..., None]
    return result.reshape(own_sources, blocks, 1, slot_width, LAGS)


def solution(mesh):
    return jax.shard_map(
        on_device,
        mesh=mesh,
        in_specs=(P("win", "chan", None), P("win", "chan")),
        out_specs=P("chan", None, "win", None, None),
        check_vma=False,
    )
```

profile of v0, /device:TPU:0, one launch (start us, length us, event | category | flops | bytes accessed | tf_op | source)
XLA Modules:
  0.0 466.3 jit_solution(18213554256155514033)
XLA Ops:
  6.5 0.0 all-gather.3.cloned.1.call-start
  6.5 0.1 multiply_subtract_fusion
  6.6 2.0 pad.6
  8.6 0.8 copy.22
  9.4 3.4 multiply_convert_fusion.2
  12.8 0.0 copy-start.2
  12.8 1.0 multiply_reduce_fusion
  13.8 0.3 copy.17
  14.2 0.0 copy-done.2
  14.2 1.2 multiply_convert_fusion
  15.4 0.0 all-gather.3.cloned.1.call-update
  15.4 0.0 all-gather.5.cloned.1.call-start
  15.5 0.7 all-gather.5.cloned.1.call-update
  16.2 25.9 %all_gather.15 = bf16[8,2048]{1,0:T(8,128)(2,1)S(1)} all-gather(bf16[8,128]{1,0:T(8,128)(2,1)S(1)} %get-tuple-element.10), channel_id=1, replica_groups=mesh['chan'=16,'win'=8] {'chan'}, dimensions={1}, use_global_device_ids=true | all-gather | bytes 34816 | tf_op jit(solution)/shard_map/all_gather | solution.py:82
  42.0 0.2 reshape.74
  42.3 0.9 reshape.78
  43.2 4.5 all-to-all-start.1
  47.7 43.3 %all-gather.3.cloned.1.call-done = bf16[8,2048,256]{2,1,0:T(8,128)(2,1)} async-done(((bf16[8,128,256]{2,1,0:T(8,128)(2,1)}), bf16[8,2048,256]{2,1,0:T(8,128)(2,1)}) %all-gather.3.cloned.1.call-update) | async-done | bytes 8388624 | tf_op jit(solution)/shard_map/all_gather | solution.py:81
  91.0 8.0 %copy.9 = bf16[8,16,8,16,256]{4,3,1,0,2:T(8,128)(2,1)} copy(bf16[8,16,8,16,256]{4,3,2,1,0:T(8,128)(2,1)} %bitcast.52) | data formatting | bytes 16777216 | tf_op jit(solution)/shard_map/reshape | solution.py:84
  99.0 0.0 all-to-all-done.1
  99.0 5.0 %all-to-all-start = ((bf16[8,16,8,16,256]{4,3,1,0,2:T(8,128)(2,1)}), bf16[8,16,8,16,256]{4,3,1,0,2:T(8,128)(2,1)}, u32[]{:S(2)}, u32[]{:S(2)}) async-start(bf16[8,16,8,16,256]{4,3,1,0,2:T(8,128)(2,1)} %copy.9), calls=%async_computation | async-start | bytes 16777216 | tf_op jit(solution)/shard_map/all_to_all | solution.py:87
  104.0 186.0 %all_gather.14 = bf16[64,128]{1,0:T(8,128)(2,1)S(1)} all-gather(bf16[8,128]{1,0:T(8,128)(2,1)S(1)} %get-tuple-element.10), channel_id=1, replica_groups=mesh['chan'=16,'win'=8] {'win'}, dimensions={0}, use_global_device_ids=true | all-gather | bytes 18432 | tf_op jit(solution)/shard_map/all_gather | solution.py:74
  290.0 0.3 fusion.14
  290.3 0.2 reshape.79
  290.6 0.2 reshape.75
  290.8 0.2 convolution_maximum_fusion
  291.0 0.0 all-gather.5.cloned.1.call-done
  291.1 4.0 fusion.20
  295.0 2.9 copy.19
  297.9 3.3 copy.21
  301.2 0.0 all-to-all-done
  301.2 6.1 %fusion.19 = (bf16[64,256,128]{2,1,0:T(8,128)(2,1)}, bf16[64,256,128]{2,1,0:T(8,128)(2,1)}) fusion(bf16[64,256,256]{2,1,0:T(8,128)(2,1)} %bitcast.6), kind=kLoop, calls=%fused_computation.39 | loop fusion | bytes 16777216 | tf_op jit(solution)/shard_map/slice | solution.py:35
  307.3 6.9 %copy.18 = bf16[64,256,128]{1,0,2:T(8,128)(2,1)} copy(bf16[64,256,128]{2,1,0:T(8,128)(2,1)} %get-tuple-element.5) | data formatting | bytes 8388608
  314.2 6.8 %copy.20 = bf16[64,256,128]{1,0,2:T(8,128)(2,1)} copy(bf16[64,256,128]{2,1,0:T(8,128)(2,1)} %get-tuple-element.6) | data formatting | bytes 8388608
  321.0 0.0 copy-start
  321.0 0.0 copy-start.1
  321.0 11.1 %fusion.22 = f32[128,256,128]{2,1,0:T(8,128)} fusion(bf16[64,256,128]{1,0,2:T(8,128)(2,1)} %copy.18, bf16[64,128,128]{1,0,2:T(8,128)(2,1)} %copy.19), kind=kOutput, calls=%fused_computation.44 | convolution fusion | flops 536870912 | bytes 23068672 | tf_op jit(solution)/shard_map/wsk,wik->sik/dot_general | solution.py:37
  332.1 0.0 copy-done
  332.1 0.0 copy-done.1
  332.1 7.5 %fusion.23 = f32[128,256,128]{2,1,0:T(8,128)} fusion(bf16[64,256,128]{1,0,2:T(8,128)(2,1)S(1)} %copy-done, bf16[64,128,128]{1,0,2:T(8,128)(2,1)S(1)} %copy-done.1), kind=kOutput, calls=%fused_computation.45 | convolution fusion | flops 536870912 | bytes 23068672 | tf_op jit(solution)/shard_map/wsk,wik->sik/dot_general | solution.py:41
  339.6 15.2 %add_bitcast_fusion = f32[128,256,128]{0,1,2:T(8,128)} fusion(f32[128,256,128]{2,1,0:T(8,128)} %fusion.22, bf16[64,256,128]{1,0,2:T(8,128)(2,1)} %copy.20, bf16[64,128,128]{1,0,2:T(8,128)(2,1)S(1)} %copy.21), kind=kOutput, calls=%fused_computation.2 | convolution fusion | flops 541065216 | bytes 39845888 | tf_op jit(solution)/shard_map/wsk,wik->sik/dot_general | solution.py:38
  354.7 15.6 %subtract_bitcast_fusion = f32[128,256,128]{0,1,2:T(8,128)} fusion(f32[128,256,128]{2,1,0:T(8,128)} %fusion.23, bf16[64,256,128]{1,0,2:T(8,128)(2,1)} %copy.18, bf16[64,128,128]{1,0,2:T(8,128)(2,1)S(1)} %copy.21), kind=kOutput, calls=%fused_computation.1 | convolution fusion | flops 541065216 | bytes 39845888 | tf_op jit(solution)/shard_map/wsk,wik->sik/dot_general | solution.py:42
  370.3 23.2 %pad_maximum_fusion = f32[128,256,256]{0,1,2:T(8,128)} fusion(f32[128,256,128]{0,1,2:T(8,128)} %subtract_bitcast_fusion, f32[128,256,128]{0,1,2:T(8,128)} %add_bitcast_fusion), kind=kLoop, calls=%fused_computation | loop fusion | flops 8388608 | bytes 67108864 | tf_op jit(solution)/shard_map/concatenate | solution.py:45
  393.5 33.6 %copy.14 = f32[128,256,256]{2,1,0:T(8,128)} copy(f32[128,256,256]{0,1,2:T(8,128)} %pad_maximum_fusion) | data formatting | bytes 67108864 | tf_op jit(solution)/shard_map/concatenate | solution.py:45
  427.1 32.4 %broadcast_divide_fusion = f32[128,256,128]{2,1,0:T(8,128)} fusion(f32[128,256]{1,0:T(8,128)S(1)} %convolution_maximum_fusion, f32[128,256,256]{2,1,0:T(8,128)} %copy.14, f32[128,128]{1,0:T(8,128)S(1)} %get-tuple-element.12, f32[128,128]{1,0:T(8,128)S(1)} %get-tuple-element.11), kind=kOutput, calls=%fused_computation.3 | convolution fusion | flops 12889128960 | bytes 50593792 | tf_op jit(solution)/shard_map/dot_general | solution.py:47
  (5 shorter events, 0.1 us)
Async XLA Ops:
  6.5 84.4 %all-gather.3.cloned.1.call-start = ((), (), s32[]{:S(2)}) async-start(), calls=%async_computation.2 | async-start | bytes 8912896 | tf_op jit(solution)/shard_map/all_gather | solution.py:81
  12.8 1.4 copy-start.2
  15.4 275.6 %all-gather.5.cloned.1.call-start = ((), (), s32[]{:S(2)}) async-start(), calls=%async_computation.3 | async-start | bytes 4718592 | tf_op jit(solution)/shard_map/all_gather | solution.py:73
  43.2 55.8 %all-to-all-start.1 = ((bf16[8,2,1024]{2,1,0:T(2,128)(2,1)}), bf16[8,2,1024]{2,1,0:T(2,128)(2,1)S(1)}, u32[]{:S(2)}, u32[]{:S(2)}) async-start(bf16[8,2,1024]{2,1,0:T(2,128)(2,1)} %reshape.78), calls=%async_computation.1 | async-start | bytes 65536 | tf_op jit(solution)/shard_map/all_to_all | solution.py:88
  99.0 202.2 %all-to-all-start = ((bf16[8,16,8,16,256]{4,3,1,0,2:T(8,128)(2,1)}), bf16[8,16,8,16,256]{4,3,1,0,2:T(8,128)(2,1)}, u32[]{:S(2)}, u32[]{:S(2)}) async-start(bf16[8,16,8,16,256]{4,3,1,0,2:T(8,128)(2,1)} %copy.9), calls=%async_computation | async-start | bytes 16777216 | tf_op jit(solution)/shard_map/all_to_all | solution.py:87
  321.0 11.1 %copy-start = (bf16[64,256,128]{1,0,2:T(8,128)(2,1)S(1)}, bf16[64,256,128]{1,0,2:T(8,128)(2,1)}, u32[]{:S(2)}) copy-start(bf16[64,256,128]{1,0,2:T(8,128)(2,1)} %copy.20) | copy-start | bytes 12582916
  321.0 11.1 %copy-start.1 = (bf16[64,128,128]{1,0,2:T(8,128)(2,1)S(1)}, bf16[64,128,128]{1,0,2:T(8,128)(2,1)}, u32[]{:S(2)}) copy-start(bf16[64,128,128]{1,0,2:T(8,128)(2,1)} %copy.19) | copy-start | bytes 6291460
Sparse Core Ops, SparseCore 0:
  15.5 75.3 all-gather.2
  92.6 159.8 all-gather.4
where the time goes:
time: 467 us; the launch traced here: 466 us
  blocking collectives  212 us (45%)
  matrix products  82.9 us (18%)
  local copies, waits for them, and re-layouts  76.3 us (16%)
  waiting for transfers between devices  44 us (9%)
  other arithmetic  28.1 us (6%)
  between operations  13.6 us (3%)
  starting transfers between devices  9.5 us (2%)
    all_gather x1, blocking collectives, on_device(): lax.all_gather(flag_half, 'win', axis=0, tiled=True)  186 us
    all_gather x1, waiting for transfers between devices, on_device(): lax.all_gather(whitened, 'chan', axis=1, tiled=True)  43.3 us
    concatenate x1, local copies, waits for them, and re-layouts, pair_block(): joined = jnp.concatenate([in_phase, quadrature], axis=-1)  33.6 us
    dot_general x1, matrix products, pair_block(): jnp.dot(joined.reshape(lead_rows * recv_rows, spec_width), inverse, preci...  32.4 us
    all_gather x1, blocking collectives, on_device(): lax.all_gather(flag_half, 'chan', axis=1, tiled=True)  25.9 us
    unnamed x14, local copies, waits for them, and re-layouts  23.8 us
    concatenate x1, other arithmetic, pair_block(): joined = jnp.concatenate([in_phase, quadrature], axis=-1)  23.2 us
    dot_general x1, matrix products, pair_block(): jnp.einsum('wsk,wik->sik', src_imag, recv_real, preferred_element_type=jn...  15.6 us
  transfers between devices with their start and end apart: 4, of which 1 were waited for; matrix products, arithmetic and copies ran while one was open for 4% of the time, Pallas kernels for 0%

commit v1 on v0

--- a/solution.py
+++ b/solution.py
@@ -78,7 +78,9 @@
     slot_width = channel_count // slot_count
     own_sources = src_spec.shape[1]
     every_spec, every_flags = (
-        lax.all_gather(whitened, "chan", axis=1, tiled=True),
+        jnp.concatenate(
+            lax.all_to_all(jnp.stack([whitened] * lax.axis_size("chan")), "chan", 0, 0), axis=1
+        ),
         lax.all_gather(flag_half, "chan", axis=1, tiled=True),
     )
     every_spec = every_spec.reshape(win_rows, blocks, slot_count, slot_width, 2 * BINS)

time: 467 us -> 516 us (1.10)
  blocking collectives: 212 us -> 300 us
  waiting for transfers between devices: 44 us -> 0.69 us
  starting transfers between devices: 9.5 us -> 18.3 us
  local copies, waits for them, and re-layouts: 76.3 us -> 70.7 us
    all_gather x1, blocking collectives: 25.9 us -> 110 us  [on_device(): lax.all_gather(flag_half, 'chan', axis=1, tiled=True)]
    all_gather x1 -> x0, waiting for transfers between devices: 43.3 us -> none  [on_device(): lax.all_gather(whitened, 'chan', axis=1, tiled=True)]
    another operation x0 -> x2, local copies, waits for them, and re-layouts: none -> 12.5 us  [the longest x1 8.01 us: on_device(): every_spec.reshape(win_rows, blocks, slot_count, slot_width, 2 * BINS)]
    reshape x2 -> x0, local copies, waits for them, and re-layouts: 8.34 us -> none  [the longest x1 8.01 us: on_device(): every_spec.reshape(win_rows, blocks, slot_count, slot_width, 2 * BINS)]
    all_to_all x0 -> x1, starting transfers between devices: none -> 8.04 us  [on_device(): lax.all_to_all(jnp.stack([whitened] * lax.axis_size('chan')), 'chan', 0, 0)]
    unnamed x14 -> x15, local copies, waits for them, and re-layouts: 23.8 us -> 17.8 us
  transfers between devices with their start and end apart: 4 -> 4, of which waited for: 1 -> 0; matrix products, arithmetic and copies ran while one was open for 4% -> 6% of each run, Pallas kernels for 0% -> 0%
where the time goes in v1:
time: 516 us; the launch traced here: 515 us
  blocking collectives  300 us (58%)
  matrix products  84 us (16%)
  local copies, waits for them, and re-layouts  70.7 us (14%)
  other arithmetic  27.2 us (5%)
  starting transfers between devices  18.3 us (4%)
  between operations  13.6 us (3%)
    all_gather x1, blocking collectives, on_device(): lax.all_gather(flag_half, 'win', axis=0, tiled=True)  191 us
    all_gather x1, blocking collectives, on_device(): lax.all_gather(flag_half, 'chan', axis=1, tiled=True)  110 us
    concatenate x1, local copies, waits for them, and re-layouts, pair_block(): joined = jnp.concatenate([in_phase, quadrature], axis=-1)  33.6 us
    dot_general x1, matrix products, pair_block(): jnp.dot(joined.reshape(lead_rows * recv_rows, spec_width), inverse, preci...  32.4 us
    concatenate x1, other arithmetic, pair_block(): joined = jnp.concatenate([in_phase, quadrature], axis=-1)  23.3 us
    unnamed x15, local copies, waits for them, and re-layouts  17.8 us
    dot_general x1, matrix products, pair_block(): jnp.einsum('wsk,wik->sik', src_imag, recv_real, preferred_element_type=jn...  16.2 us
    dot_general x1, matrix products, pair_block(): jnp.einsum('wsk,wik->sik', src_imag, recv_imag, preferred_element_type=jn...  15.7 us
  transfers between devices with their start and end apart: 4, of which 0 were waited for; matrix products, arithmetic and copies ran while one was open for 6% of the time, Pallas kernels for 0%

profile of v1, /device:TPU:0, one launch (start us, length us, event | category | flops | bytes accessed | tf_op | source)
XLA Modules:
  0.0 514.8 jit_solution(16679361346861991136)
XLA Ops:
  6.5 0.1 multiply_subtract_fusion
  6.6 2.0 pad.6
  8.6 0.8 copy.26
  9.4 3.4 multiply_convert_fusion.1
  12.8 0.0 copy-start.3
  12.8 1.0 fusion.8
  13.8 0.2 copy.27
  14.1 0.0 copy-done.3
  14.1 0.1 fusion.7
  14.2 0.0 copy-start.2
  14.2 0.3 copy.15
  14.6 4.4 stack.2
  19.0 0.0 copy-done.2
  19.0 8.0 %all-to-all-start = ((bf16[16,8,128,256]{3,2,1,0:T(8,128)(2,1)}), bf16[16,8,128,256]{3,2,1,0:T(8,128)(2,1)}, u32[]{:S(2)}, u32[]{:S(2)}) async-start(bf16[16,8,128,256]{3,2,1,0:T(8,128)(2,1)} %stack.2), calls=%async_computation | async-start | bytes 16777216 | tf_op jit(solution)/shard_map/all_to_all | solution.py:82
  27.1 109.6 %all_gather.11 = bf16[8,2048]{1,0:T(8,128)(2,1)S(1)} all-gather(bf16[8,128]{1,0:T(8,128)(2,1)S(1)} %get-tuple-element.8), channel_id=1, replica_groups=mesh['chan'=16,'win'=8] {'chan'}, dimensions={1}, use_global_device_ids=true | all-gather | bytes 34816 | tf_op jit(solution)/shard_map/all_gather | solution.py:84
  136.6 0.2 reshape.77
  136.9 0.9 reshape.81
  137.8 0.0 all-to-all-done
  137.8 4.5 all-to-all-start.2
  142.3 8.0 %copy.17 = bf16[8,16,8,16,256]{4,3,1,0,2:T(8,128)(2,1)} copy(bf16[8,16,8,16,256]{4,3,2,0,1:T(8,128)(2,1)} %bitcast.4) | data formatting | bytes 16777216 | tf_op jit(solution)/shard_map/reshape;reshape | solution.py:86
  150.3 0.0 all-to-all-done.2
  150.3 5.7 %all-to-all-start.1 = ((bf16[8,16,8,16,256]{4,3,1,0,2:T(8,128)(2,1)}), bf16[8,16,8,16,256]{4,3,1,0,2:T(8,128)(2,1)}, u32[]{:S(2)}, u32[]{:S(2)}) async-start(bf16[8,16,8,16,256]{4,3,1,0,2:T(8,128)(2,1)} %copy.17), calls=%async_computation.1 | async-start | bytes 16777216 | tf_op jit(solution)/shard_map/all_to_all | solution.py:89
  156.0 0.0 all-gather.2.cloned.1.call-start
  156.0 0.7 all-gather.2.cloned.1.call-update
  156.7 190.7 %all_gather.10 = bf16[64,128]{1,0:T(8,128)(2,1)S(1)} all-gather(bf16[8,128]{1,0:T(8,128)(2,1)S(1)} %get-tuple-element.8), channel_id=1, replica_groups=mesh['chan'=16,'win'=8] {'win'}, dimensions={0}, use_global_device_ids=true | all-gather | bytes 18432 | tf_op jit(solution)/shard_map/all_gather | solution.py:74
  347.4 0.3 fusion.24
  347.8 0.2 reshape.82
  348.0 0.2 reshape.78
  348.3 0.2 convolution_maximum_fusion
  348.5 0.0 all-to-all-done.1
  348.5 6.0 %fusion.29 = (bf16[64,256,128]{2,1,0:T(8,128)(2,1)}, bf16[64,256,128]{2,1,0:T(8,128)(2,1)}) fusion(bf16[64,256,256]{2,1,0:T(8,128)(2,1)} %bitcast.7), kind=kLoop, calls=%fused_computation.48 | loop fusion | bytes 16777216 | tf_op jit(solution)/shard_map/slice | solution.py:35
  354.5 6.8 %copy.24 = bf16[64,256,128]{1,0,2:T(8,128)(2,1)} copy(bf16[64,256,128]{2,1,0:T(8,128)(2,1)} %get-tuple-element.5) | data formatting | bytes 8388608
  361.3 6.9 %copy.25 = bf16[64,256,128]{1,0,2:T(8,128)(2,1)} copy(bf16[64,256,128]{2,1,0:T(8,128)(2,1)} %get-tuple-element.6) | data formatting | bytes 8388608
  368.2 0.0 all-gather.2.cloned.1.call-done
  368.2 0.0 copy-start
  368.2 0.0 copy-start.1
  368.2 11.1 %fusion.4 = f32[128,256,128]{2,1,0:T(8,128)} fusion(bf16[64,256,128]{1,0,2:T(8,128)(2,1)} %copy.24, bf16[64,128,256]{1,0,2:T(8,128)(2,1)} %all-gather.2.cloned.1.call-done), kind=kOutput, calls=%fused_computation.8 | convolution fusion | flops 536870912 | bytes 23068672 | tf_op jit(solution)/shard_map/wsk,wik->sik/dot_general | solution.py:37
  379.3 0.0 copy-done
  379.3 0.0 copy-done.1
  379.3 7.5 %fusion.2 = f32[128,256,128]{2,1,0:T(8,128)} fusion(bf16[64,256,128]{1,0,2:T(8,128)(2,1)S(1)} %copy-done, bf16[64,128,256]{1,0,2:T(8,128)(2,1)S(1)} %copy-done.1), kind=kOutput, calls=%fused_computation.6 | convolution fusion | flops 536870912 | bytes 23068672 | tf_op jit(solution)/shard_map/wsk,wik->sik/dot_general | solution.py:41
  386.7 15.7 %add_bitcast_fusion = f32[128,256,128]{0,1,2:T(8,128)} fusion(f32[128,256,128]{2,1,0:T(8,128)} %fusion.4, bf16[64,256,128]{1,0,2:T(8,128)(2,1)} %copy.25, bf16[64,128,256]{1,0,2:T(8,128)(2,1)} %all-gather.2.cloned.1.call-done), kind=kOutput, calls=%fused_computation.2 | convolution fusion | flops 541065216 | bytes 39845888 | tf_op jit(solution)/shard_map/wsk,wik->sik/dot_general | solution.py:38
  402.5 16.2 %subtract_bitcast_fusion = f32[128,256,128]{0,1,2:T(8,128)} fusion(f32[128,256,128]{2,1,0:T(8,128)} %fusion.2, bf16[64,256,128]{1,0,2:T(8,128)(2,1)} %copy.24, bf16[64,128,256]{1,0,2:T(8,128)(2,1)} %all-gather.2.cloned.1.call-done), kind=kOutput, calls=%fused_computation.1 | convolution fusion | flops 541065216 | bytes 39845888 | tf_op jit(solution)/shard_map/wsk,wik->sik/dot_general | solution.py:42
  418.6 23.3 %pad_maximum_fusion = f32[128,256,256]{0,1,2:T(8,128)} fusion(f32[128,256,128]{0,1,2:T(8,128)} %subtract_bitcast_fusion, f32[128,256,128]{0,1,2:T(8,128)} %add_bitcast_fusion), kind=kLoop, calls=%fused_computation | loop fusion | flops 8388608 | bytes 67108864 | tf_op jit(solution)/shard_map/concatenate | solution.py:45
  441.9 33.6 %copy.20 = f32[128,256,256]{2,1,0:T(8,128)} copy(f32[128,256,256]{0,1,2:T(8,128)} %pad_maximum_fusion) | data formatting | bytes 67108864 | tf_op jit(solution)/shard_map/concatenate | solution.py:45
  475.5 32.4 %broadcast_divide_fusion = f32[128,256,128]{2,1,0:T(8,128)} fusion(f32[128,256]{1,0:T(8,128)S(1)} %convolution_maximum_fusion, f32[128,256,256]{2,1,0:T(8,128)} %copy.20, f32[128,128]{1,0:T(8,128)S(1)} %get-tuple-element.10, f32[128,128]{1,0:T(8,128)S(1)} %get-tuple-element.9), kind=kOutput, calls=%fused_computation.3 | convolution fusion | flops 12889128960 | bytes 50593792 | tf_op jit(solution)/shard_map/dot_general | solution.py:47
  (5 shorter events, 0.1 us)
Async XLA Ops:
  12.8 1.3 copy-start.3
  14.2 4.8 copy-start.2
  19.0 118.8 %all-to-all-start = ((bf16[16,8,128,256]{3,2,1,0:T(8,128)(2,1)}), bf16[16,8,128,256]{3,2,1,0:T(8,128)(2,1)}, u32[]{:S(2)}, u32[]{:S(2)}) async-start(bf16[16,8,128,256]{3,2,1,0:T(8,128)(2,1)} %stack.2), calls=%async_computation | async-start | bytes 16777216 | tf_op jit(solution)/shard_map/all_to_all | solution.py:82
  137.8 12.5 %all-to-all-start.2 = ((bf16[8,2,1024]{2,1,0:T(2,128)(2,1)}), bf16[8,2,1024]{2,1,0:T(2,128)(2,1)S(1)}, u32[]{:S(2)}, u32[]{:S(2)}) async-start(bf16[8,2,1024]{2,1,0:T(2,128)(2,1)} %reshape.81), calls=%async_computation.2 | async-start | bytes 65536 | tf_op jit(solution)/shard_map/all_to_all | solution.py:90
  150.3 198.2 %all-to-all-start.1 = ((bf16[8,16,8,16,256]{4,3,1,0,2:T(8,128)(2,1)}), bf16[8,16,8,16,256]{4,3,1,0,2:T(8,128)(2,1)}, u32[]{:S(2)}, u32[]{:S(2)}) async-start(bf16[8,16,8,16,256]{4,3,1,0,2:T(8,128)(2,1)} %copy.17), calls=%async_computation.1 | async-start | bytes 16777216 | tf_op jit(solution)/shard_map/all_to_all | solution.py:89
  156.0 212.2 %all-gather.2.cloned.1.call-start = ((), (), s32[]{:S(2)}) async-start(), calls=%async_computation.3 | async-start | bytes 4718592 | tf_op jit(solution)/shard_map/all_gather | solution.py:73
  368.2 11.1 %copy-start = (bf16[64,256,128]{1,0,2:T(8,128)(2,1)S(1)}, bf16[64,256,128]{1,0,2:T(8,128)(2,1)}, u32[]{:S(2)}) copy-start(bf16[64,256,128]{1,0,2:T(8,128)(2,1)} %copy.25) | copy-start | bytes 12582916
  368.2 11.1 %copy-start.1 = (bf16[64,128,256]{1,0,2:T(8,128)(2,1)S(1)}, bf16[64,128,256]{1,0,2:T(8,128)(2,1)}, u32[]{:S(2)}) copy-start(bf16[64,128,256]{1,0,2:T(8,128)(2,1)} %all-gather.2.cloned.1.call-done) | copy-start | bytes 12582916
Sparse Core Ops, SparseCore 0:
  158.4 166.8 all-gather.1
